TPU v7x, 32 devices: a whole 2x2x4 slice. The times are simulated.
32 devices in a mesh: row: 4 (over y, x), col: 8 (over z, core).
Axes of the slice: x: 2, y: 2, z: 4, core: 2. Of those that a mesh axis runs over, the one named last changes fastest.
Arguments:
- parent_front: bfloat16 [28672, 28672], P('row', 'col'), may hold values from -6 to 6
- child_update: bfloat16 [2, 14336, 14336], P(None, 'row', 'col'), may hold values from -6 to 6
- parent_test: bfloat16 [28672, 448], P('col'), may hold values from -0.03125 to 0.03125
- child_test: bfloat16 [2, 14336, 448], P(None, 'col'), may hold values from -0.046875 to 0.046875
- child_map: int32 [2, 112], replicated, may hold values from 0 to 223, as said below
Outputs:
- leaf_basis: bfloat16 [224, 128, 448], P('row', 'col')
- couplings: float32 [32, 448, 448], P('row', 'col')
Inputs may be any that keep to these rules, and one draw needn't show every extreme that they name: `child_map`: for each child the entries rise strictly along its blocks, and entry j is at least j.
All inputs are finite; a program needn't handle non-finite values.
Results may differ from a plain program's by a relative error of at most 0.006.
Values may be sent and summed in bfloat16 or wider, within the bound.
A program may use at most 192 MiB of HBM per device.

v0:
```python
import math
import jax
import jax.numpy as jnp
from jax import lax
from jax.sharding import PartitionSpec as P

LEAF = 896
BLOCK = 128
HIGH = lax.Precision.HIGHEST


def spread(block, axis, holder):
    block = jnp.where(lax.axis_index(axis) == holder, block, jnp.zeros_like(block))
    return lax.psum(block, axis)


def finish(leaves, gram_matrix):
    factor = jnp.linalg.cholesky(gram_matrix)
    solved = lax.linalg.triangular_solve(
        factor, leaves, left_side=False, lower=True, transpose_a=True
    )
    return (solved * math.sqrt(LEAF)).astype(jnp.bfloat16)


def local(parent_front, child_update, parent_test, child_test, child_map):
    row_count = lax.axis_size("row")
    col_count = lax.axis_size("col")
    row_index = lax.axis_index("row")
    col_index = lax.axis_index("col")
    slab_rows = BLOCK // col_count
    own_blocks = parent_front.shape[0] // BLOCK
    kid_blocks = child_update.shape[1] // BLOCK
    probes = parent_test.shape[1]
    own_probe = jnp.dot(parent_front, parent_test, preferred_element_type=jnp.float32)
    own_probe = own_probe.reshape(own_blocks, BLOCK, probes)
    kid_probe = jnp.stack(
        [
            jnp.dot(child_update[which], child_test[which], preferred_element_type=jnp.float32)
            for which in range(2)
        ]
    )
    kid_probe = kid_probe.reshape(2, kid_blocks, BLOCK, probes)
    own_share, kid_share = (
        lax.psum_scatter(own_probe, "col", scatter_dimension=1, tiled=True),
        lax.psum_scatter(kid_probe, "col", scatter_dimension=2, tiled=True),
    )
    first_block = row_index * own_blocks
    targets = jnp.arange(own_blocks, dtype=jnp.int32)
    mapped = child_map - first_block
    onehot = (mapped[:, None, :] == targets[None, :, None]).astype(jnp.float32)
    sample = own_share + jnp.einsum(
        "cpn,cnsr->psr",
        onehot,
        lax.all_gather(kid_share, "row", axis=1, tiled=True),
        precision=HIGH,
    )
    per_leaf = LEAF // BLOCK
    leaf_count = own_blocks // per_leaf
    leaves = sample.reshape(leaf_count, per_leaf * slab_rows, probes)
    partial_gram = jnp.einsum("lkr,lks->lrs", leaves, leaves, precision=HIGH)
    gram_matrix = lax.psum(partial_gram, "col")
    leaf_basis = finish(leaves, gram_matrix).reshape(own_blocks, slab_rows, probes)
    whole_basis = lax.all_gather(leaf_basis, "col", axis=1, tiled=True)
    bases = whole_basis.reshape(leaf_count, LEAF, probes)
    col_leaves = parent_front.shape[1] // LEAF
    shrink = 1.0 / math.sqrt(LEAF)

    def sibling_product(position):
        leaf_index = col_index * col_leaves + position
        sibling = jnp.bitwise_xor(leaf_index, 1)
        row_start = leaf_index % leaf_count * LEAF
        col_start = (sibling - col_index * col_leaves) * LEAF
        front_tile = lax.dynamic_slice(parent_front, (row_start, col_start), (LEAF, LEAF))
        product = (
            jnp.dot(front_tile, bases[sibling % leaf_count], preferred_element_type=jnp.float32)
            * shrink
        )
        return product.astype(jnp.bfloat16)

    products = lax.map(sibling_product, jnp.arange(col_leaves, dtype=jnp.int32))
    owner_span = col_count // row_count
    core_rows = probes // col_count
    received = [
        spread(products, "col", row_index * owner_span + offset) for offset in range(owner_span)
    ]
    products_all = jnp.concatenate(received, axis=0)
    columns = lax.dynamic_slice_in_dim(bases, col_index * core_rows, core_rows, 2)
    couplings = (
        jnp.einsum("lkr,lks->lrs", columns, products_all, preferred_element_type=jnp.float32)
        * shrink
    )
    return (leaf_basis, couplings)


def solution(mesh):
    in_specs = (P("row", "col"), P(None, "row", "col"), P("col", None), P(None, "col", None), P())
    out_specs = (P("row", "col", None), P("row", "col", None))
    return jax.shard_map(local, mesh=mesh, in_specs=in_specs, out_specs=out_specs, check_vma=False)
```

profile of v0, /device:TPU:0, one launch (start us, length us, event | category | flops | bytes accessed | tf_op | source)
XLA Modules:
  0.0 1988.0 jit_solution(7997422557833170795)
XLA Ops:
  7.2 9.5 fusion.77
  16.7 10.6 convolution_bitcast_fusion.1
  27.3 10.6 convolution_bitcast_fusion.2
  37.8 10.9 pad_maximum_fusion
  48.7 21.7 %copy.91 = f32[2,28,128,448]{3,0,1,2:T(2,128)} copy(f32[2,28,128,448]{2,3,1,0:T(8,128)} %pad_maximum_fusion) | data formatting | bytes 25690112 | tf_op jit(solution)/shard_map/stack | solution.py:36
  72.3 295.1 %all-reduce.11.cloned.1.call-done = f32[2,28,128,448]{3,0,1,2:T(2,128)} async-done(((f32[2,28,128,448]{3,0,1,2:T(2,128)}), f32[2,28,128,448]{3,0,1,2:T(2,128)}) %all-reduce.11.cloned.1.call-update) | async-done | bytes 12845072
  372.4 30.3 %convolution_bitcast_fusion = f32[56,8,56,128]{3,1,2,0:T(8,128)} fusion(bf16[7168,3584]{1,0:T(8,128)(2,1)} %param.7, bf16[3584,448]{0,1:T(8,128)(2,1)S(1)} %copy-done), kind=kOutput, calls=%fused_computation.11 | convolution fusion | flops 23018340352 | bytes 67436544 | tf_op jit(solution)/shard_map/dot_general | solution.py:34
  402.7 12.1 copy.136
  414.8 16.4 copy.90
  431.9 19.0 all-gather.3.cloned.1.call-done
  450.9 151.3 %reduce-scatter.2.cloned.1.call-done = f32[56,16,448]{2,0,1:T(8,128)} async-done(((f32[56,128,448]{2,0,1:T(8,128)}), f32[56,16,448]{2,0,1:T(8,128)}) %reduce-scatter.2.cloned.1.call-update) | async-done | bytes 1605648 | tf_op jit(solution)/shard_map/reduce_scatter | solution.py:44
  602.2 10.3 bitcast_add_fusion.1
  613.6 8.1 fusion.78
  623.1 153.0 %all-reduce.9.cloned.1.call-done = f32[8,448,448]{1,2,0:T(8,128)} async-done(((f32[8,448,448]{1,2,0:T(8,128)}), f32[8,448,448]{1,2,0:T(8,128)}) %all-reduce.9.cloned.1.call-update) | async-done | bytes 6422544 | tf_op jit(solution)/shard_map/psum | solution.py:61
  776.1 8.5 copy.97
  784.6 7.0 fusion.13
  791.6 2.9 copy-done.3
  794.6 93.8 %custom-call.34 = f32[8,128,128]{2,1,0:T(8,128)S(1)} custom-call(f32[8,128,128]{2,1,0:T(8,128)S(1)} %cholesky.281), custom_call_target="Cholesky" | custom-call | tf_op jit(solution)/shard_map/jit(cholesky)/cholesky | solution.py:18
  888.4 4.0 cholesky.236
  892.4 79.2 %custom-call.35 = f32[8,1,128,128]{2,3,1,0:T(8,128)} custom-call(f32[8,1,128,128]{3,2,1,0:T(8,128)S(1)} %select_bitcast_fusion.2), custom_call_target="InvertDiagBlocksLowerTriangular" | custom-call | tf_op jit(solution)/shard_map/jit(cholesky)/cholesky | solution.py:18
  971.7 3.9 constant_dynamic-update-slice_fusion.3
  975.5 2.7 convolution_subtract_fusion
  979.3 94.2 %custom-call.36 = f32[8,128,128]{2,1,0:T(8,128)S(1)} custom-call(f32[8,128,128]{2,1,0:T(8,128)S(1)} %cholesky.285), custom_call_target="Cholesky" | custom-call | tf_op jit(solution)/shard_map/jit(cholesky)/cholesky | solution.py:18
  1074.5 79.2 %custom-call.37 = f32[8,1,128,128]{2,3,1,0:T(8,128)} custom-call(f32[8,1,128,128]{3,2,1,0:T(8,128)S(1)} %get-tuple-element.154), custom_call_target="InvertDiagBlocksLowerTriangular" | custom-call | tf_op jit(solution)/shard_map/jit(cholesky)/cholesky | solution.py:18
  1153.8 3.1 convolution_dynamic-update-slice_fusion
  1156.9 3.6 fusion.38
  1161.3 95.4 %custom-call.38 = f32[8,128,128]{2,1,0:T(8,128)} custom-call(f32[8,128,128]{2,1,0:T(8,128)} %cholesky.290), custom_call_target="Cholesky" | custom-call | tf_op jit(solution)/shard_map/jit(cholesky)/cholesky | solution.py:18
  1259.1 79.4 %custom-call.39 = f32[8,1,128,128]{2,3,1,0:T(8,128)S(1)} custom-call(f32[8,1,128,128]{3,2,1,0:T(8,128)} %get-tuple-element.152), custom_call_target="InvertDiagBlocksLowerTriangular" | custom-call | tf_op jit(solution)/shard_map/jit(cholesky)/cholesky | solution.py:18
  1339.8 2.5 convolution_subtract_fusion.3
  1342.4 46.9 %custom-call.40 = f32[8,64,64]{2,1,0:T(8,128)S(1)} custom-call(f32[8,64,64]{2,1,0:T(8,128)S(1)} %convolution_subtract_fusion.3), custom_call_target="Cholesky" | custom-call | tf_op jit(solution)/shard_map/jit(cholesky)/cholesky | solution.py:18
  1390.4 4.3 select_select_fusion
  1394.8 2.9 copy-done.2
  1397.7 12.5 while.16
  1398.3 3.6 bitcast_dynamic-update-slice_fusion.3
  1402.4 3.6 bitcast_dynamic-update-slice_fusion.3
  1406.6 3.6 bitcast_dynamic-update-slice_fusion.3
  1410.5 3.0 pad_maximum_fusion.1
  1413.5 316.0 %custom-call.41 = f32[8,4,128,128]{2,3,1,0:T(8,128)} custom-call(f32[8,4,128,128]{3,2,1,0:T(8,128)} %pad_maximum_fusion.1), custom_call_target="InvertDiagBlocksLowerTriangular" | custom-call | tf_op jit(solution)/shard_map/triangular_solve | solution.py:19
  1737.2 3.1 fusion.41
  1742.5 73.5 %all-gather.5.cloned.1.call-done = bf16[56,128,448]{2,1,0:T(8,128)(2,1)} async-done(((bf16[56,16,448]{2,1,0:T(8,128)(2,1)}), bf16[56,128,448]{2,1,0:T(8,128)(2,1)}) %all-gather.5.cloned.1.call-update) | async-done | bytes 6422544 | tf_op jit(solution)/shard_map/all_gather | solution.py:63
  1816.0 17.0 while.15
  1817.6 2.8 fusion.100
  1821.7 2.8 fusion.100
  1825.9 2.9 fusion.100
  1830.2 2.8 fusion.100
  1833.0 3.2 broadcast_select_fusion.1
  1836.2 137.2 %all-reduce.13.cloned.1.call-done = (bf16[4,896,448]{1,2,0:T(8,128)(2,1)}, bf16[4,896,448]{1,2,0:T(8,128)(2,1)}) async-done(((bf16[4,896,448]{1,2,0:T(8,128)(2,1)}, bf16[4,896,448]{1,2,0:T(8,128)(2,1)}), (bf16[4,896,448]{1,2,0:T(8,128)(2,1)}, bf16[4,896,448]{1,2,0:T(8,128)(2,1)})) %all-reduce.13.cloned.1.call-update) | async-done | bytes 6422544 | tf_op jit(solution)/shard_map/psum | solution.py:14
  1973.5 7.4 fusion.52
  (82 shorter events, 31.6 us)
Async XLA Ops:
  7.2 365.2 %copy-start = (bf16[3584,448]{0,1:T(8,128)(2,1)S(1)}, bf16[3584,448]{0,1:T(8,128)(2,1)}, u32[]{:S(2)}) copy-start(bf16[3584,448]{0,1:T(8,128)(2,1)} %param.9) | copy-start | bytes 9633796
  7.2 360.2 %all-reduce.11.cloned.1.call-start = ((), (), s32[]{:S(2)}) async-start(), calls=%async_computation.5 | async-start | bytes 29360128
  70.4 0.7 copy-start.10
  70.4 380.5 %all-gather.3.cloned.1.call-start = ((), (), s32[]{:S(2)}) async-start(), calls=%async_computation.2 | async-start | bytes 9175040 | tf_op jit(solution)/shard_map/all_gather | solution.py:54
  371.8 230.4 %reduce-scatter.2.cloned.1.call-start = ((), (), s32[]{:S(2)}) async-start(), calls=%async_computation.1 | async-start | bytes 16515072 | tf_op jit(solution)/shard_map/reduce_scatter | solution.py:44
  431.2 0.7 copy-start.9
  431.2 344.9 %all-reduce.9.cloned.1.call-start = ((), (), s32[]{:S(2)}) async-start(), calls=%async_computation.3 | async-start | bytes 14680064 | tf_op jit(solution)/shard_map/psum | solution.py:61
  621.7 1194.3 %all-gather.5.cloned.1.call-start = ((), (), s32[]{:S(2)}) async-start(), calls=%async_computation.4 | async-start | bytes 8257536 | tf_op jit(solution)/shard_map/all_gather | solution.py:63
  791.6 2.9 copy-start.3
  888.4 4.0 copy-start.5
  978.2 1.1 copy-start.4
  1073.5 80.2 %copy-start.7 = (f32[8,128,128]{2,1,0:T(8,128)}, f32[8,128,128]{2,1,0:T(8,128)S(1)}, u32[]{:S(2)}) copy-start(f32[8,128,128]{2,1,0:T(8,128)S(1)} %custom-call.36) | copy-start | bytes 1572868
  1153.8 102.9 %copy-start.6 = (f32[8,128,128]{2,1,0:T(8,128)S(1)}, f32[8,128,128]{2,1,0:T(8,128)}, u32[]{:S(2)}) copy-start(f32[8,128,128]{2,1,0:T(8,128)} %copy-done.5) | copy-start | bytes 1572868
  1394.7 2.9 copy-start.2
  1729.5 4.1 copy-start.8
  1742.4 231.1 %all-reduce.13.cloned.1.call-start = ((), (), s32[]{:S(2)}) async-start(), calls=%async_computation.6 | async-start | bytes 12845056 | tf_op jit(solution)/shard_map/psum | solution.py:14
  1973.5 7.4 copy-start.1
Sparse Core Ops, SparseCore 0:
  70.5 296.7 all-reduce.10
  371.9 78.9 all-gather.2
  453.2 148.9 reduce-scatter.1
  621.9 154.2 all-reduce.8
  1742.5 73.4 all-gather.4
  1836.3 137.0 all-reduce.12
where the time goes:
time: 2000 us; the launch traced here: 1990 us
  other arithmetic  919 us (46%)
  waiting for transfers between devices  829 us (41%)
  matrix products  118 us (6%)
  local copies, waits for them, and re-layouts  102 us (5%)
    another operation x18, other arithmetic, finish(): factor = jnp.linalg.cholesky(gram_matrix)  573 us
    another operation x8, other arithmetic, finish(): lax.linalg.triangular_solve(factor, leaves, left_side=False, lower=True,...  324 us
    unnamed x7, waiting for transfers between devices  295 us
    psum x1, waiting for transfers between devices, local(): gram_matrix = lax.psum(partial_gram, 'col')  153 us
    reduce_scatter x1, waiting for transfers between devices, local(): lax.psum_scatter(own_probe, 'col', scatter_dimension=1, tiled=True)  151 us
    psum x1, waiting for transfers between devices, spread(): return lax.psum(block, axis)  137 us
    all_gather x1, waiting for transfers between devices, local(): whole_basis = lax.all_gather(leaf_basis, 'col', axis=1, tiled=True)  73.5 us
  transfers between devices with their start and end apart: 6, of which 6 were waited for; matrix products, arithmetic and copies ran while one was open for 3% of the time, Pallas kernels for 0%

commit v1 on v0

--- a/solution.py
+++ b/solution.py
@@ -7,6 +7,11 @@
 LEAF = 896
 BLOCK = 128
 HIGH = lax.Precision.HIGHEST
+
+
+def switch_chains(mine_x):
+    even = lax.all_gather(mine_x, axis_name="col").sum(axis=0)
+    return even
 
 
 def spread(block, axis, holder):
@@ -58,7 +63,7 @@
     leaf_count = own_blocks // per_leaf
     leaves = sample.reshape(leaf_count, per_leaf * slab_rows, probes)
     partial_gram = jnp.einsum("lkr,lks->lrs", leaves, leaves, precision=HIGH)
-    gram_matrix = lax.psum(partial_gram, "col")
+    gram_matrix = switch_chains(partial_gram)
     leaf_basis = finish(leaves, gram_matrix).reshape(own_blocks, slab_rows, probes)
     whole_basis = lax.all_gather(leaf_basis, "col", axis=1, tiled=True)
     bases = whole_basis.reshape(leaf_count, LEAF, probes)

time: 2000 us -> 2360 us (1.18)
  waiting for transfers between devices: 829 us -> 1170 us
    all_gather x0 -> x1, waiting for transfers between devices: none -> 493 us  [switch_chains(): even = lax.all_gather(mine_x, axis_name='col').sum(axis=0)]
    psum x1 -> x0, waiting for transfers between devices: 153 us -> none  [local(): gram_matrix = lax.psum(partial_gram, 'col')]
where the time goes in v1:
time: 2360 us; the launch traced here: 2350 us
  waiting for transfers between devices  1170 us (50%)
  other arithmetic  941 us (40%)
  matrix products  117 us (5%)
  local copies, waits for them, and re-layouts  102 us (4%)
    another operation x18, other arithmetic, finish(): factor = jnp.linalg.cholesky(gram_matrix)  572 us
    all_gather x1, waiting for transfers between devices, switch_chains(): even = lax.all_gather(mine_x, axis_name='col').sum(axis=0)  493 us
    another operation x8, other arithmetic, finish(): lax.linalg.triangular_solve(factor, leaves, left_side=False, lower=True,...  324 us
    unnamed x7, waiting for transfers between devices  295 us
    reduce_scatter x1, waiting for transfers between devices, local(): lax.psum_scatter(own_probe, 'col', scatter_dimension=1, tiled=True)  151 us
    psum x1, waiting for transfers between devices, spread(): return lax.psum(block, axis)  137 us
    all_gather x1, waiting for transfers between devices, local(): whole_basis = lax.all_gather(leaf_basis, 'col', axis=1, tiled=True)  71.6 us
  transfers between devices with their start and end apart: 6, of which 6 were waited for; matrix products, arithmetic and copies ran while one was open for 3% of the time, Pallas kernels for 0%

profile of v1, /device:TPU:0, one launch (start us, length us, event | category | flops | bytes accessed | tf_op | source)
XLA Modules:
  0.0 2347.9 jit_solution(12527099344854173640)
XLA Ops:
  7.2 9.5 fusion.77
  16.7 10.6 convolution_bitcast_fusion.1
  27.3 10.6 convolution_bitcast_fusion.2
  37.8 10.9 pad_maximum_fusion
  48.7 21.7 copy.87
  72.3 295.1 %all-reduce.8.cloned.1.call-done = f32[2,28,128,448]{3,0,1,2:T(2,128)} async-done(((f32[2,28,128,448]{3,0,1,2:T(2,128)}), f32[2,28,128,448]{3,0,1,2:T(2,128)}) %all-reduce.8.cloned.1.call-update) | async-done | bytes 12845072
  372.1 30.3 %convolution_bitcast_fusion = f32[56,8,56,128]{3,1,2,0:T(8,128)} fusion(bf16[7168,3584]{1,0:T(8,128)(2,1)} %param.7, bf16[3584,448]{0,1:T(8,128)(2,1)S(1)} %copy-done), kind=kOutput, calls=%fused_computation.11 | convolution fusion | flops 23018340352 | bytes 67436544 | tf_op jit(solution)/shard_map/dot_general | solution.py:39
  402.4 12.2 copy.131
  414.6 16.4 copy.86
  431.7 19.2 all-gather.5.cloned.1.call-done
  450.9 151.3 %reduce-scatter.2.cloned.1.call-done = f32[56,16,448]{2,0,1:T(8,128)} async-done(((f32[56,128,448]{2,0,1:T(8,128)}), f32[56,16,448]{2,0,1:T(8,128)}) %reduce-scatter.2.cloned.1.call-update) | async-done | bytes 1605648 | tf_op jit(solution)/shard_map/reduce_scatter | solution.py:49
  602.2 10.3 bitcast_add_fusion.1
  613.7 8.0 fusion.78
  623.3 492.5 %all-gather.9.cloned.1.call-done = f32[64,448,448]{2,1,0:T(8,128)} async-done(((f32[8,448,448]{2,1,0:T(8,128)}), f32[64,448,448]{2,1,0:T(8,128)}) %all-gather.9.cloned.1.call-update) | async-done | bytes 51380240 | tf_op jit(solution)/shard_map/all_gather | solution.py:13
  1115.8 22.0 reduce_sum.9
  1137.9 8.5 copy.92
  1146.4 7.0 fusion.13
  1153.4 2.9 copy-done.3
  1156.4 93.8 %custom-call.34 = f32[8,128,128]{2,1,0:T(8,128)S(1)} custom-call(f32[8,128,128]{2,1,0:T(8,128)S(1)} %cholesky.281), custom_call_target="Cholesky" | custom-call | tf_op jit(solution)/shard_map/jit(cholesky)/cholesky | solution.py:23
  1250.2 4.0 cholesky.236
  1254.2 79.4 %custom-call.35 = f32[8,1,128,128]{2,3,1,0:T(8,128)} custom-call(f32[8,1,128,128]{3,2,1,0:T(8,128)S(1)} %select_bitcast_fusion.2), custom_call_target="InvertDiagBlocksLowerTriangular" | custom-call | tf_op jit(solution)/shard_map/jit(cholesky)/cholesky | solution.py:23
  1333.6 3.9 constant_dynamic-update-slice_fusion.3
  1337.5 2.7 convolution_subtract_fusion
  1341.3 93.8 %custom-call.36 = f32[8,128,128]{2,1,0:T(8,128)S(1)} custom-call(f32[8,128,128]{2,1,0:T(8,128)S(1)} %cholesky.285), custom_call_target="Cholesky" | custom-call | tf_op jit(solution)/shard_map/jit(cholesky)/cholesky | solution.py:23
  1436.1 79.2 %custom-call.37 = f32[8,1,128,128]{2,3,1,0:T(8,128)} custom-call(f32[8,1,128,128]{3,2,1,0:T(8,128)S(1)} %get-tuple-element.154), custom_call_target="InvertDiagBlocksLowerTriangular" | custom-call | tf_op jit(solution)/shard_map/jit(cholesky)/cholesky | solution.py:23
  1515.3 3.1 convolution_dynamic-update-slice_fusion
  1518.4 3.6 fusion.38
  1522.8 95.4 %custom-call.38 = f32[8,128,128]{2,1,0:T(8,128)} custom-call(f32[8,128,128]{2,1,0:T(8,128)} %cholesky.290), custom_call_target="Cholesky" | custom-call | tf_op jit(solution)/shard_map/jit(cholesky)/cholesky | solution.py:23
  1620.6 79.4 %custom-call.39 = f32[8,1,128,128]{2,3,1,0:T(8,128)S(1)} custom-call(f32[8,1,128,128]{3,2,1,0:T(8,128)} %get-tuple-element.152), custom_call_target="InvertDiagBlocksLowerTriangular" | custom-call | tf_op jit(solution)/shard_map/jit(cholesky)/cholesky | solution.py:23
  1703.9 46.9 %custom-call.40 = f32[8,64,64]{2,1,0:T(8,128)S(1)} custom-call(f32[8,64,64]{2,1,0:T(8,128)S(1)} %convolution_subtract_fusion.3), custom_call_target="Cholesky" | custom-call | tf_op jit(solution)/shard_map/jit(cholesky)/cholesky | solution.py:23
  1752.0 4.3 select_select_fusion
  1756.4 2.9 copy-done.2
  1759.3 12.5 while.16
  1759.9 3.6 bitcast_dynamic-update-slice_fusion.3
  1764.0 3.6 bitcast_dynamic-update-slice_fusion.3
  1768.2 3.6 bitcast_dynamic-update-slice_fusion.3
  1772.0 3.0 pad_maximum_fusion.1
  1775.0 316.1 %custom-call.41 = f32[8,4,128,128]{2,3,1,0:T(8,128)} custom-call(f32[8,4,128,128]{3,2,1,0:T(8,128)} %pad_maximum_fusion.1), custom_call_target="InvertDiagBlocksLowerTriangular" | custom-call | tf_op jit(solution)/shard_map/triangular_solve | solution.py:24
  2098.8 3.1 fusion.41
  2104.1 71.6 %all-gather.7.cloned.1.call-done = bf16[56,128,448]{2,1,0:T(8,128)(2,1)} async-done(((bf16[56,16,448]{2,1,0:T(8,128)(2,1)}), bf16[56,128,448]{2,1,0:T(8,128)(2,1)}) %all-gather.7.cloned.1.call-update) | async-done | bytes 6422544 | tf_op jit(solution)/shard_map/all_gather | solution.py:68
  2175.7 17.0 while.15
  2177.3 2.8 fusion.100
  2181.5 2.8 fusion.100
  2185.7 2.8 fusion.100
  2189.8 2.8 fusion.100
  2192.7 3.2 broadcast_select_fusion.1
  2195.9 137.2 %all-reduce.10.cloned.1.call-done = (bf16[4,896,448]{1,2,0:T(8,128)(2,1)}, bf16[4,896,448]{1,2,0:T(8,128)(2,1)}) async-done(((bf16[4,896,448]{1,2,0:T(8,128)(2,1)}, bf16[4,896,448]{1,2,0:T(8,128)(2,1)}), (bf16[4,896,448]{1,2,0:T(8,128)(2,1)}, bf16[4,896,448]{1,2,0:T(8,128)(2,1)})) %all-reduce.10.cloned.1.call-update) | async-done | bytes 6422544 | tf_op jit(solution)/shard_map/psum | solution.py:19
  2333.1 7.4 fusion.52
  (83 shorter events, 34.1 us)
Async XLA Ops:
  7.2 364.9 %copy-start = (bf16[3584,448]{0,1:T(8,128)(2,1)S(1)}, bf16[3584,448]{0,1:T(8,128)(2,1)}, u32[]{:S(2)}) copy-start(bf16[3584,448]{0,1:T(8,128)(2,1)} %param.9) | copy-start | bytes 9633796
  7.2 360.2 %all-reduce.8.cloned.1.call-start = ((), (), s32[]{:S(2)}) async-start(), calls=%async_computation.5 | async-start | bytes 29360128
  70.4 0.7 copy-start.10
  70.4 380.5 %all-gather.5.cloned.1.call-start = ((), (), s32[]{:S(2)}) async-start(), calls=%async_computation.2 | async-start | bytes 9175040 | tf_op jit(solution)/shard_map/all_gather | solution.py:59
  371.8 230.4 %reduce-scatter.2.cloned.1.call-start = ((), (), s32[]{:S(2)}) async-start(), calls=%async_computation.1 | async-start | bytes 16515072 | tf_op jit(solution)/shard_map/reduce_scatter | solution.py:49
  431.1 0.7 copy-start.9
  431.1 684.8 %all-gather.9.cloned.1.call-start = ((), (), s32[]{:S(2)}) async-start(), calls=%async_computation.4 | async-start | bytes 66060288 | tf_op jit(solution)/shard_map/all_gather | solution.py:13
  621.7 1554.0 %all-gather.7.cloned.1.call-start = ((), (), s32[]{:S(2)}) async-start(), calls=%async_computation.3 | async-start | bytes 8257536 | tf_op jit(solution)/shard_map/all_gather | solution.py:68
  1153.4 2.9 copy-start.3
  1250.2 4.0 copy-start.5
  1340.2 1.1 copy-start.4
  1435.1 80.2 %copy-start.7 = (f32[8,128,128]{2,1,0:T(8,128)}, f32[8,128,128]{2,1,0:T(8,128)S(1)}, u32[]{:S(2)}) copy-start(f32[8,128,128]{2,1,0:T(8,128)S(1)} %custom-call.36) | copy-start | bytes 1572868
  1515.3 103.0 %copy-start.6 = (f32[8,128,128]{2,1,0:T(8,128)S(1)}, f32[8,128,128]{2,1,0:T(8,128)}, u32[]{:S(2)}) copy-start(f32[8,128,128]{2,1,0:T(8,128)} %copy-done.5) | copy-start | bytes 1572868
  1756.3 2.9 copy-start.2
  2091.1 4.1 copy-start.8
  2104.0 229.1 %all-reduce.10.cloned.1.call-start = ((), (), s32[]{:S(2)}) async-start(), calls=%async_computation.6 | async-start | bytes 12845056 | tf_op jit(solution)/shard_map/psum | solution.py:19
  2333.1 7.4 copy-start.1
Sparse Core Ops, SparseCore 0:
  70.5 296.7 all-reduce.7
  371.9 78.9 all-gather.4
  453.3 148.9 reduce-scatter.1
  621.8 493.9 all-gather.8
  2104.1 71.5 all-gather.6
  2196.0 137.0 all-reduce.9
